TPU v7x, 512 devices: a whole 4x4x16 slice. The times are simulated.
512 devices in a mesh: seg: 64 (over z, x), sub: 8 (over y, core).
Axes of the slice: x: 4, y: 4, z: 16, core: 2. Of those that a mesh axis runs over, the one named last changes fastest.
Arguments:
- near_blocks: bfloat16 [1024, 10, 256, 256], P(('seg', 'sub')), may hold values from -0.375 to 0.375
- sample_cols: bfloat16 [262144, 256], P(('seg', 'sub')), may hold values from -6 to 6
- near_list: int32 [1024, 10], P(('seg', 'sub')), may hold values from -1 to 1023, as said below
- row_basis_t: bfloat16 [1024, 64, 256], P(('seg', 'sub')), may hold values from -0.75 to 0.75
- col_basis_t: bfloat16 [1024, 64, 256], P(('seg', 'sub')), may hold values from -0.375 to 0.375
- couplings: bfloat16 [64, 8, 64, 64, 128], P('seg', 'sub'), may hold values from -0.125 to 0.125
- far_source: int32 [64, 8, 64, 2], P('seg', 'sub'), may hold values from 0 to 2
- far_dest: int32 [64, 8, 64, 2], P('seg', 'sub'), may hold values from 0 to 1
Outputs:
- samples: bfloat16 [262144, 256], P(('seg', 'sub'))
- segment_factor: float32 [16384, 256], P('seg')
- transfers: bfloat16 [64, 3, 256, 256], P('seg')
Inputs may be any that keep to these rules, and one draw needn't show every extreme that they name: `near_list`: entry 0 of every list is the leaf itself; -1 marks padding and stands only after the real entries; every other entry names a leaf held by the same device or by the device just before or just after it in the order of seg, then sub. `far_source`: entry [s', u, s, c] is the local leaf of device (s', u) whose far projection fills slot c toward device (s, u); the value 2 marks an empty slot. `far_dest`: entry [s, u, s', c] is the local leaf of device (s, u) that slot c from device (s', u) serves.
All inputs are finite; a program needn't handle non-finite values.
Results may differ from a plain program's by a relative error of at most 0.013.
Values may be sent and summed in bfloat16 or wider, within the bound.
A program may use at most 64 MiB of HBM per device.

v0:
```python
import jax
import jax.numpy as jnp
from jax import lax
from jax.sharding import PartitionSpec as P

LEVELS = 3


def padded(value, sides, width):
    for axis, dim in sides:
        size, length = (lax.axis_size(axis), value.shape[dim])
        up = [(i, (i + 1) % size) for i in range(size - 1)]
        down = [(j, i) for i, j in up]
        last = lax.slice_in_dim(value, length - width, length, axis=dim)
        leading = lax.slice_in_dim(value, 0, width, axis=dim)
        before = lax.ppermute(last, axis, up)
        after = lax.ppermute(leading, axis, down)
        value = jnp.concatenate([before, value, after], axis=dim)
    return value


def from_partner(value, axis, distance):
    mask = 2**distance
    pairs = [(source, source ^ mask) for source in range(lax.axis_size(axis))]
    return lax.ppermute(value, axis, pairs)


def body(
    near_blocks, sample_cols, near_list, row_basis_t, col_basis_t, couplings, far_source, far_dest
):
    leaf_count, near_count, leaf_rows, _ = near_blocks.shape
    sample_width = sample_cols.shape[1]
    rank_width = row_basis_t.shape[1]
    seg_count = lax.axis_size("seg")
    slot_number_count = far_source.shape[3]
    random_cols = sample_cols.reshape(leaf_count, leaf_rows, sample_width)
    basis_projector = jnp.einsum(
        "jra,jas->jrs", col_basis_t, random_cols, preferred_element_type=jnp.float32
    ).astype(jnp.bfloat16)
    extended = padded(sample_cols, ((("seg", "sub"), 0),), leaf_count * leaf_rows)
    extended = extended.reshape(3 * leaf_count, leaf_rows, sample_width)
    base_leaf = (lax.axis_index(("seg", "sub")) - 1) * leaf_count
    usable = near_list >= 0
    position = jnp.where(usable, near_list - base_leaf, 0)
    chosen = extended[position]
    chosen = jnp.where(usable[:, :, None, None], chosen, jnp.zeros_like(chosen))
    near_part = jnp.einsum(
        "lkab,lkbs->las", near_blocks, chosen, preferred_element_type=jnp.float32
    )
    leaf_range = jnp.arange(leaf_count, dtype=jnp.int32)
    routing = far_dest[0, 0][:, :, None] == leaf_range[None, None, :]
    coupling_set = jnp.transpose(
        couplings[0, 0].reshape(seg_count, rank_width, slot_number_count, rank_width), (1, 0, 2, 3)
    )
    masked = jnp.where(
        jnp.transpose(routing, (2, 0, 1))[:, None, :, :, None],
        coupling_set[None],
        jnp.zeros((), jnp.bfloat16),
    )
    masked = masked.reshape(leaf_count * rank_width, seg_count * slot_number_count * rank_width)
    selection_choice = (far_source[0, 0][:, :, None] == leaf_range[None, None, :]).astype(
        jnp.bfloat16
    )
    outgoing = jnp.einsum(
        "zgy,ykf->zgkf", selection_choice, basis_projector, preferred_element_type=jnp.float32
    ).astype(jnp.bfloat16)
    incoming = lax.all_to_all(outgoing, "seg", split_axis=0, concat_axis=0, tiled=True)
    far_total = jnp.dot(
        masked,
        incoming.reshape(seg_count * slot_number_count * rank_width, sample_width),
        preferred_element_type=jnp.float32,
    )
    far_coeff = far_total.astype(jnp.bfloat16).reshape(leaf_count, rank_width, sample_width)
    distant_portion = jnp.einsum(
        "lra,lrs->las", row_basis_t, far_coeff, preferred_element_type=jnp.float32
    )
    samples = (
        (near_part + distant_portion)
        .astype(jnp.bfloat16)
        .reshape(leaf_count * leaf_rows, sample_width)
    )
    gram_local = lax.dot_general(
        samples, samples, (((0,), (0,)), ((), ())), preferred_element_type=jnp.float32
    )
    row_total = lax.axis_size("sub") * leaf_count * leaf_rows
    current = lax.psum(gram_local.astype(jnp.bfloat16), "sub").astype(jnp.float32) / row_total
    gram_levels = [current]
    for segment_position_index in range(LEVELS):
        partner = from_partner(current.astype(jnp.bfloat16), "seg", segment_position_index).astype(
            current.dtype
        )
        current = (current + partner) * 0.5
        gram_levels.append(current)
    stacked = jnp.stack(gram_levels)
    triangles = jnp.linalg.cholesky(stacked)
    segment_factor = jnp.swapaxes(triangles[0], 0, 1)
    solved = jax.vmap(
        lambda upper_one, lower_one: jax.scipy.linalg.solve_triangular(
            upper_one, lower_one, lower=True
        )
    )(triangles[1:], triangles[:-1])
    transfers = jnp.swapaxes(solved, 1, 2).astype(jnp.bfloat16)[None]
    return (samples, segment_factor, transfers)


def solution(mesh):
    in_specs = (
        P(("seg", "sub"), None, None, None),
        P(("seg", "sub"), None),
        P(("seg", "sub"), None),
        P(("seg", "sub"), None, None),
        P(("seg", "sub"), None, None),
        P("seg", "sub", None, None, None),
        P("seg", "sub", None, None),
        P("seg", "sub", None, None),
    )
    out_specs = (P(("seg", "sub"), None), P("seg", None), P("seg", None, None, None))
    return jax.shard_map(body, mesh=mesh, in_specs=in_specs, out_specs=out_specs, check_vma=False)
```

profile of v0, /device:TPU:2, one launch (start us, length us, event | category | flops | bytes accessed | tf_op | source)
XLA Modules:
  0.0 559.7 jit_solution(11103013563132528204)
XLA Ops:
  10.5 4.4 copy.66
  14.9 19.0 %all-to-all-start = ((bf16[64,2,64,256]{3,2,1,0:T(8,128)(2,1)}), bf16[64,2,64,256]{3,2,1,0:T(8,128)(2,1)}, u32[]{:S(2)}, u32[]{:S(2)}) async-start(bf16[64,2,64,256]{3,2,1,0:T(8,128)(2,1)} %copy.66), calls=%async_computation | async-start | bytes 8388608 | tf_op jit(solution)/shard_map/all_to_all | solution.py:67
  35.8 5.8 %collective-permute-start.1 = (bf16[512,256]{1,0:T(8,128)(2,1)S(1)}, bf16[512,256]{1,0:T(8,128)(2,1)}, u32[]{:S(2)}, u32[]{:S(2)}) collective-permute-start(bf16[512,256]{1,0:T(8,128)(2,1)S(1)} %copy-done.4), channel_id=1, source_target_pairs={{1,0},{2,1},{3,2},{4,3},{5,4},{6,5},{7,6},{8,7},{9,8},{10,9},{11,1... | collective-permute-start | bytes 786440 | tf_op jit(solution)/shard_map/ppermute | solution.py:17
  41.7 5.3 reshape_squeeze.3
  47.1 4.0 copy.95
  53.4 12.6 %copy.64 = bf16[2,64,64,2,64]{4,3,2,1,0:T(2,128)(2,1)} copy(bf16[2,64,64,2,64]{4,2,3,1,0:T(8,128)(2,1)} %broadcast_select_fusion) | data formatting | bytes 4194304 | tf_op jit(solution)/shard_map/jit(_where)/select_n | solution.py:55
  66.0 21.4 %select_n.33 = bf16[128,8192]{1,0:T(8,128)(2,1)} reshape(bf16[2,64,64,2,64]{4,3,2,1,0:T(2,128)(2,1)} %copy.64) | data formatting | bytes 4194304 | tf_op jit(solution)/shard_map/jit(_where)/select_n | solution.py:55
  89.3 2.4 gather_fusion
  91.7 2.6 fusion.4
  94.4 129.4 %all-to-all-done = bf16[64,2,64,256]{3,2,1,0:T(8,128)(2,1)} async-done(((bf16[64,2,64,256]{3,2,1,0:T(8,128)(2,1)}), bf16[64,2,64,256]{3,2,1,0:T(8,128)(2,1)}, u32[]{:S(2)}, u32[]{:S(2)}) %all-to-all-start) | async-done | bytes 4194336 | tf_op jit(solution)/shard_map/all_to_all | solution.py:67
  223.8 3.6 convolution_convert_fusion.2
  229.3 76.0 %all-reduce.3.cloned.1.call-done = bf16[256,256]{0,1:T(8,128)(2,1)} async-done(((bf16[256,256]{0,1:T(8,128)(2,1)}), bf16[256,256]{0,1:T(8,128)(2,1)}) %all-reduce.3.cloned.1.call-update) | async-done | bytes 131088 | tf_op jit(solution)/shard_map/psum | solution.py:86
  306.2 2.5 collective-permute-start.2
  308.7 4.4 collective-permute-done.2
  314.1 4.0 collective-permute-start.3
  318.7 3.7 collective-permute-done.3
  323.5 3.5 collective-permute-start.4
  328.1 2.3 collective-permute-done.4
  333.3 2.5 copy.69
  338.3 46.9 %custom-call.17 = f32[4,128,128]{2,1,0:T(8,128)S(1)} custom-call(f32[4,128,128]{2,1,0:T(8,128)S(1)} %cholesky.122), custom_call_target="Cholesky" | custom-call | tf_op jit(solution)/shard_map/jit(cholesky)/cholesky | solution.py:95
  386.3 39.3 %custom-call.18 = f32[4,1,128,128]{2,3,1,0:T(8,128)S(1)} custom-call(f32[4,1,128,128]{3,2,1,0:T(8,128)S(1)} %select_bitcast_fusion), custom_call_target="InvertDiagBlocksLowerTriangular" | custom-call | tf_op jit(solution)/shard_map/jit(cholesky)/cholesky | solution.py:95
  429.4 46.9 %custom-call.19 = f32[4,128,128]{2,1,0:T(8,128)S(1)} custom-call(f32[4,128,128]{2,1,0:T(8,128)S(1)} %convolution_subtract_fusion.1), custom_call_target="Cholesky" | custom-call | tf_op jit(solution)/shard_map/jit(cholesky)/cholesky | solution.py:95
  480.4 5.4 while.1
  485.8 60.4 %custom-call.20 = f32[3,2,128,128]{2,3,1,0:T(8,128)} custom-call(f32[3,2,128,128]{3,2,1,0:T(8,128)} %bitcast.101), custom_call_target="InvertDiagBlocksLowerTriangular" | custom-call | tf_op jit(solution)/shard_map/vmap(jit(_solve_triangular))/triangular_solve | solution.py:98
  (81 shorter events, 42.2 us)
Async XLA Ops:
  7.2 84.6 %copy-start = (bf16[2,10,256,256]{3,2,1,0:T(8,128)(2,1)S(1)}, bf16[2,10,256,256]{3,2,1,0:T(8,128)(2,1)}, u32[]{:S(2)}) copy-start(bf16[2,10,256,256]{3,2,1,0:T(8,128)(2,1)} %param.8) | copy-start | bytes 7864324
  14.9 19.0 %copy-start.4 = (bf16[512,256]{1,0:T(8,128)(2,1)S(1)}, bf16[512,256]{1,0:T(8,128)(2,1)}, u32[]{:S(2)}) copy-start(bf16[512,256]{1,0:T(8,128)(2,1)} %param.9) | copy-start | bytes 786436
  14.9 26.7 %copy-start.13 = (s32[2,10]{1,0:T(2,128)S(1)}, s32[2,10]{1,0:T(2,128)}, u32[]{:S(2)}) copy-start(s32[2,10]{1,0:T(2,128)} %param.10) | copy-start | bytes 244
  14.9 208.9 %all-to-all-start = ((bf16[64,2,64,256]{3,2,1,0:T(8,128)(2,1)}), bf16[64,2,64,256]{3,2,1,0:T(8,128)(2,1)}, u32[]{:S(2)}, u32[]{:S(2)}) async-start(bf16[64,2,64,256]{3,2,1,0:T(8,128)(2,1)} %copy.66), calls=%async_computation | async-start | bytes 8388608 | tf_op jit(solution)/shard_map/all_to_all | solution.py:67
  33.9 271.5 %all-reduce.3.cloned.1.call-start = ((), (), s32[]{:S(2)}) async-start(), calls=%async_computation.1 | async-start | bytes 262144 | tf_op jit(solution)/shard_map/psum | solution.py:86
  33.9 53.5 %collective-permute-start = (bf16[512,256]{1,0:T(8,128)(2,1)S(1)}, bf16[512,256]{1,0:T(8,128)(2,1)S(1)}, u32[]{:S(2)}, u32[]{:S(2)}) collective-permute-start(bf16[512,256]{1,0:T(8,128)(2,1)S(1)} %copy-done.4), channel_id=1, source_target_pairs={{0,1},{1,2},{2,3},{3,4},{4,5},{5,6},{6,7},{7,8},{8,9},{9,10},{10,1... | collective-permute-start | bytes 786440 | tf_op jit(solution)/shard_map/ppermute | solution.py:16
  35.8 52.3 %collective-permute-start.1 = (bf16[512,256]{1,0:T(8,128)(2,1)S(1)}, bf16[512,256]{1,0:T(8,128)(2,1)}, u32[]{:S(2)}, u32[]{:S(2)}) collective-permute-start(bf16[512,256]{1,0:T(8,128)(2,1)S(1)} %copy-done.4), channel_id=1, source_target_pairs={{1,0},{2,1},{3,2},{4,3},{5,4},{6,5},{7,6},{8,7},{9,8},{10,9},{11,1... | collective-permute-start | bytes 786440 | tf_op jit(solution)/shard_map/ppermute | solution.py:17
  47.1 4.0 copy-start.12
  87.4 0.7 copy-start.9
  223.8 3.6 copy-start.10
  227.6 0.7 copy-start.8
  306.2 6.9 %collective-permute-start.2 = (bf16[256,256]{0,1:T(8,128)(2,1)S(1)}, bf16[256,256]{0,1:T(8,128)(2,1)S(1)}, u32[]{:S(2)}, u32[]{:S(2)}) collective-permute-start(bf16[256,256]{0,1:T(8,128)(2,1)S(1)} %fusion.16), channel_id=1, source_target_pairs={{0,8},{8,0},{16,24},{24,16},{32,40},{40,32},{48,56},{56,48},{64,72... | collective-permute-start | bytes 393224 | tf_op jit(solution)/shard_map/ppermute | solution.py:25
  314.1 8.4 %collective-permute-start.3 = (bf16[256,256]{0,1:T(8,128)(2,1)S(1)}, bf16[256,256]{0,1:T(8,128)(2,1)S(1)}, u32[]{:S(2)}, u32[]{:S(2)}) collective-permute-start(bf16[256,256]{0,1:T(8,128)(2,1)S(1)} %get-tuple-element.44), channel_id=1, source_target_pairs={{0,16},{8,24},{16,0},{24,8},{32,48},{40,56},{48,32},{56,40},{64,80... | collective-permute-start | bytes 393224 | tf_op jit(solution)/shard_map/ppermute | solution.py:25
  322.4 5.7 %copy-start.6 = (bf16[256,256]{0,1:T(8,128)(2,1)}, bf16[256,256]{0,1:T(8,128)(2,1)S(1)}, u32[]{:S(2)}) copy-start(bf16[256,256]{0,1:T(8,128)(2,1)S(1)} %collective-permute-done.3) | copy-start | bytes 393220
  323.5 7.0 %collective-permute-start.4 = (bf16[256,256]{0,1:T(8,128)(2,1)S(1)}, bf16[256,256]{0,1:T(8,128)(2,1)}, u32[]{:S(2)}, u32[]{:S(2)}) collective-permute-start(bf16[256,256]{0,1:T(8,128)(2,1)S(1)} %get-tuple-element.39), channel_id=1, source_target_pairs={{0,32},{8,40},{16,48},{24,56},{32,0},{40,8},{48,16},{56,24},{64,96... | collective-permute-start | bytes 393224 | tf_op jit(solution)/shard_map/ppermute | solution.py:25
  331.6 0.7 copy-start.3
  335.9 50.4 %copy-start.11 = (pred[128,128]{1,0:T(8,128)(4,1)S(1)}, pred[128,128]{1,0:T(8,128)(4,1)}, u32[]{:S(2)}) copy-start(pred[128,128]{1,0:T(8,128)(4,1)} %iota_compare_fusion.1) | copy-start | bytes 49156
  337.3 1.0 copy-start.2
  338.3 138.9 %copy-start.5 = (pred[256,256]{1,0:T(8,128)(4,1)S(1)}, pred[256,256]{1,0:T(8,128)(4,1)}, u32[]{:S(2)}) copy-start(pred[256,256]{1,0:T(8,128)(4,1)} %iota_compare_fusion) | copy-start | bytes 196612
  429.4 51.0 %copy-start.14 = (s32[2]{0:T(128)S(1)}, s32[2]{0:T(128)}, u32[]{:S(2)}) copy-start(s32[2]{0:T(128)} %iota_multiply_fusion) | copy-start | bytes 28
  478.6 1.0 copy-start.1
  546.2 3.2 copy-start.7
Sparse Core Ops, SparseCore 0:
  229.4 75.8 all-reduce.2
where the time goes:
time: 566 us; the launch traced here: 560 us
  waiting for transfers between devices  216 us (38%)
  other arithmetic  208 us (37%)
  local copies, waits for them, and re-layouts  66.8 us (12%)
  starting transfers between devices  36.6 us (6%)
  matrix products  18.1 us (3%)
  between operations  14.6 us (3%)
    another operation x9, other arithmetic, body(): triangles = jnp.linalg.cholesky(stacked)  135 us
    all_to_all x1, waiting for transfers between devices, body(): lax.all_to_all(outgoing, 'seg', split_axis=0, concat_axis=0, tiled=True)  129 us
    psum x1, waiting for transfers between devices, body(): lax.psum(gram_local.astype(jnp.bfloat16), 'sub').astype(jnp.float32)  76 us
    another operation x3, other arithmetic, body(): jax.scipy.linalg.solve_triangular(upper_one, lower_one, lower=True)  61 us
    select_n x2, local copies, waits for them, and re-layouts, body(): jnp.where(jnp.transpose(routing, (2, 0, 1))[:, None, :, :, None], couplin...  34 us
    all_to_all x1, starting transfers between devices, body(): lax.all_to_all(outgoing, 'seg', split_axis=0, concat_axis=0, tiled=True)  19 us
  transfers between devices with their start and end apart: 7, of which 5 were waited for; matrix products, arithmetic and copies ran while one was open for 10% of the time, Pallas kernels for 0%

commit v1 on v0

--- a/solution.py
+++ b/solution.py
@@ -83,7 +83,10 @@
         samples, samples, (((0,), (0,)), ((), ())), preferred_element_type=jnp.float32
     )
     row_total = lax.axis_size("sub") * leaf_count * leaf_rows
-    current = lax.psum(gram_local.astype(jnp.bfloat16), "sub").astype(jnp.float32) / row_total
+    current = (
+        jnp.sum(lax.all_gather(gram_local.astype(jnp.bfloat16), "sub"), axis=0).astype(jnp.float32)
+        / row_total
+    )
     gram_levels = [current]
     for segment_position_index in range(LEVELS):
         partner = from_partner(current.astype(jnp.bfloat16), "seg", segment_position_index).astype(

time: 566 us -> 522 us (0.922)
  waiting for transfers between devices: 216 us -> 172 us
    psum x1 -> x0, waiting for transfers between devices: 76 us -> none  [body(): lax.psum(gram_local.astype(jnp.bfloat16), 'sub').astype(jnp.float32)]
    all_gather x0 -> x1, waiting for transfers between devices: none -> 31.5 us  [body(): lax.all_gather(gram_local.astype(jnp.bfloat16), 'sub')]
where the time goes in v1:
time: 522 us; the launch traced here: 516 us
  other arithmetic  207 us (40%)
  waiting for transfers between devices  172 us (33%)
  local copies, waits for them, and re-layouts  67.6 us (13%)
  starting transfers between devices  36.8 us (7%)
  matrix products  18.1 us (3%)
  between operations  14.6 us (3%)
    another operation x9, other arithmetic, body(): triangles = jnp.linalg.cholesky(stacked)  135 us
    all_to_all x1, waiting for transfers between devices, body(): lax.all_to_all(outgoing, 'seg', split_axis=0, concat_axis=0, tiled=True)  129 us
    another operation x3, other arithmetic, body(): jax.scipy.linalg.solve_triangular(upper_one, lower_one, lower=True)  61 us
    select_n x2, local copies, waits for them, and re-layouts, body(): jnp.where(jnp.transpose(routing, (2, 0, 1))[:, None, :, :, None], couplin...  34.1 us
    all_gather x1, waiting for transfers between devices, body(): lax.all_gather(gram_local.astype(jnp.bfloat16), 'sub')  31.5 us
    all_to_all x1, starting transfers between devices, body(): lax.all_to_all(outgoing, 'seg', split_axis=0, concat_axis=0, tiled=True)  19 us
    ppermute x3, waiting for transfers between devices, from_partner(): return lax.ppermute(value, axis, pairs)  10.9 us
  transfers between devices with their start and end apart: 7, of which 5 were waited for; matrix products, arithmetic and copies ran while one was open for 10% of the time, Pallas kernels for 0%

profile of v1, /device:TPU:2, one launch (start us, length us, event | category | flops | bytes accessed | tf_op | source)
XLA Modules:
  0.0 515.8 jit_solution(15624283908412215658)
XLA Ops:
  10.5 4.4 copy.64
  14.9 19.0 %all-to-all-start = ((bf16[64,2,64,256]{3,2,1,0:T(8,128)(2,1)}), bf16[64,2,64,256]{3,2,1,0:T(8,128)(2,1)}, u32[]{:S(2)}, u32[]{:S(2)}) async-start(bf16[64,2,64,256]{3,2,1,0:T(8,128)(2,1)} %copy.64), calls=%async_computation | async-start | bytes 8388608 | tf_op jit(solution)/shard_map/all_to_all | solution.py:67
  35.8 5.8 %collective-permute-start.1 = (bf16[512,256]{1,0:T(8,128)(2,1)S(1)}, bf16[512,256]{1,0:T(8,128)(2,1)}, u32[]{:S(2)}, u32[]{:S(2)}) collective-permute-start(bf16[512,256]{1,0:T(8,128)(2,1)S(1)} %copy-done.5), channel_id=1, source_target_pairs={{1,0},{2,1},{3,2},{4,3},{5,4},{6,5},{7,6},{8,7},{9,8},{10,9},{11,1... | collective-permute-start | bytes 786440 | tf_op jit(solution)/shard_map/ppermute | solution.py:17
  41.7 5.3 %reshape_squeeze.3 = bf16[64,64,2,64]{3,2,1,0:T(2,128)(2,1)} reshape(bf16[1,1,64,64,128]{4,3,2,1,0:T(8,128)(2,1)} %param.13) | data formatting | bytes 2097152 | tf_op jit(solution)/shard_map/reshape;squeeze | solution.py:53
  47.1 4.0 copy.91
  53.4 12.6 %copy.62 = bf16[2,64,64,2,64]{4,3,2,1,0:T(2,128)(2,1)} copy(bf16[2,64,64,2,64]{4,2,3,1,0:T(8,128)(2,1)} %broadcast_select_fusion) | data formatting | bytes 4194304 | tf_op jit(solution)/shard_map/jit(_where)/select_n | solution.py:55
  66.0 21.5 %select_n.33 = bf16[128,8192]{1,0:T(8,128)(2,1)} reshape(bf16[2,64,64,2,64]{4,3,2,1,0:T(2,128)(2,1)} %copy.62) | data formatting | bytes 4194304 | tf_op jit(solution)/shard_map/jit(_where)/select_n | solution.py:55
  89.4 2.4 gather_fusion
  91.9 2.7 fusion.4
  94.5 129.3 %all-to-all-done = bf16[64,2,64,256]{3,2,1,0:T(8,128)(2,1)} async-done(((bf16[64,2,64,256]{3,2,1,0:T(8,128)(2,1)}), bf16[64,2,64,256]{3,2,1,0:T(8,128)(2,1)}, u32[]{:S(2)}, u32[]{:S(2)}) %all-to-all-start) | async-done | bytes 4194336 | tf_op jit(solution)/shard_map/all_to_all | solution.py:67
  223.8 3.6 convolution_convert_fusion.2
  229.3 31.5 %all-gather.3.cloned.1.call-done = bf16[2048,256]{1,0:T(8,128)(2,1)} async-done(((bf16[256,256]{1,0:T(8,128)(2,1)}), bf16[2048,256]{1,0:T(8,128)(2,1)}) %all-gather.3.cloned.1.call-update) | async-done | bytes 1048592 | tf_op jit(solution)/shard_map/all_gather | solution.py:87
  262.3 2.6 collective-permute-start.2
  265.0 4.9 collective-permute-done.2
  269.9 4.0 collective-permute-start.3
  274.5 3.7 collective-permute-done.3
  278.9 3.5 collective-permute-start.4
  283.6 2.3 collective-permute-done.4
  288.8 2.5 copy.67
  293.7 46.9 %custom-call.17 = f32[4,128,128]{2,1,0:T(8,128)S(1)} custom-call(f32[4,128,128]{2,1,0:T(8,128)S(1)} %cholesky.122), custom_call_target="Cholesky" | custom-call | tf_op jit(solution)/shard_map/jit(cholesky)/cholesky | solution.py:98
  342.5 39.3 %custom-call.18 = f32[4,1,128,128]{2,3,1,0:T(8,128)S(1)} custom-call(f32[4,1,128,128]{3,2,1,0:T(8,128)S(1)} %select_bitcast_fusion), custom_call_target="InvertDiagBlocksLowerTriangular" | custom-call | tf_op jit(solution)/shard_map/jit(cholesky)/cholesky | solution.py:98
  385.5 46.9 %custom-call.19 = f32[4,128,128]{2,1,0:T(8,128)S(1)} custom-call(f32[4,128,128]{2,1,0:T(8,128)S(1)} %convolution_subtract_fusion.1), custom_call_target="Cholesky" | custom-call | tf_op jit(solution)/shard_map/jit(cholesky)/cholesky | solution.py:98
  436.5 5.4 %while.1 = (s32[]{:T(128)}, f32[3,256,256]{2,1,0:T(8,128)S(1)}, s32[2,2]{1,0:T(2,128)S(1)}, f32[2,3,128,128]{3,2,0,1:T(8,128)}, s32[]{:T(128)}) while((s32[]{:T(128)}, f32[3,256,256]{2,1,0:T(8,128)S(1)}, s32[2,2]{1,0:T(2,128)S(1)}, f32[2,3,128,128]{3,2,0,1:T(8,128)}, s32[]{:T(128)}) %tuple.36), condition=%wide.while_cond, body=%wide.while_body.sunk | while | flops 2 | bytes 394849 | solution.py:101
  441.9 60.4 %custom-call.20 = f32[3,2,128,128]{2,3,1,0:T(8,128)} custom-call(f32[3,2,128,128]{3,2,1,0:T(8,128)} %bitcast.103), custom_call_target="InvertDiagBlocksLowerTriangular" | custom-call | tf_op jit(solution)/shard_map/vmap(jit(_solve_triangular))/triangular_solve | solution.py:101
  (83 shorter events, 42.1 us)
Async XLA Ops:
  7.2 84.7 %copy-start = (bf16[2,10,256,256]{3,2,1,0:T(8,128)(2,1)S(1)}, bf16[2,10,256,256]{3,2,1,0:T(8,128)(2,1)}, u32[]{:S(2)}) copy-start(bf16[2,10,256,256]{3,2,1,0:T(8,128)(2,1)} %param.8) | copy-start | bytes 7864324
  14.9 19.0 %copy-start.5 = (bf16[512,256]{1,0:T(8,128)(2,1)S(1)}, bf16[512,256]{1,0:T(8,128)(2,1)}, u32[]{:S(2)}) copy-start(bf16[512,256]{1,0:T(8,128)(2,1)} %param.9) | copy-start | bytes 786436
  14.9 26.7 %copy-start.13 = (s32[2,10]{1,0:T(2,128)S(1)}, s32[2,10]{1,0:T(2,128)}, u32[]{:S(2)}) copy-start(s32[2,10]{1,0:T(2,128)} %param.10) | copy-start | bytes 244
  14.9 208.9 %all-to-all-start = ((bf16[64,2,64,256]{3,2,1,0:T(8,128)(2,1)}), bf16[64,2,64,256]{3,2,1,0:T(8,128)(2,1)}, u32[]{:S(2)}, u32[]{:S(2)}) async-start(bf16[64,2,64,256]{3,2,1,0:T(8,128)(2,1)} %copy.64), calls=%async_computation | async-start | bytes 8388608 | tf_op jit(solution)/shard_map/all_to_all | solution.py:67
  33.9 226.9 %all-gather.3.cloned.1.call-start = ((), (), s32[]{:S(2)}) async-start(), calls=%async_computation.1 | async-start | bytes 1179648 | tf_op jit(solution)/shard_map/all_gather | solution.py:87
  33.9 53.6 %collective-permute-start = (bf16[512,256]{1,0:T(8,128)(2,1)S(1)}, bf16[512,256]{1,0:T(8,128)(2,1)S(1)}, u32[]{:S(2)}, u32[]{:S(2)}) collective-permute-start(bf16[512,256]{1,0:T(8,128)(2,1)S(1)} %copy-done.5), channel_id=1, source_target_pairs={{0,1},{1,2},{2,3},{3,4},{4,5},{5,6},{6,7},{7,8},{8,9},{9,10},{10,1... | collective-permute-start | bytes 786440 | tf_op jit(solution)/shard_map/ppermute | solution.py:16
  35.8 52.4 %collective-permute-start.1 = (bf16[512,256]{1,0:T(8,128)(2,1)S(1)}, bf16[512,256]{1,0:T(8,128)(2,1)}, u32[]{:S(2)}, u32[]{:S(2)}) collective-permute-start(bf16[512,256]{1,0:T(8,128)(2,1)S(1)} %copy-done.5), channel_id=1, source_target_pairs={{1,0},{2,1},{3,2},{4,3},{5,4},{6,5},{7,6},{8,7},{9,8},{10,9},{11,1... | collective-permute-start | bytes 786440 | tf_op jit(solution)/shard_map/ppermute | solution.py:17
  47.1 4.0 copy-start.12
  87.5 0.7 copy-start.10
  223.8 3.6 copy-start.11
  227.6 0.7 copy-start.9
  262.3 7.5 %collective-permute-start.2 = (bf16[256,256]{0,1:T(8,128)(2,1)S(1)}, bf16[256,256]{0,1:T(8,128)(2,1)S(1)}, u32[]{:S(2)}, u32[]{:S(2)}) collective-permute-start(bf16[256,256]{0,1:T(8,128)(2,1)S(1)} %fusion.16), channel_id=1, source_target_pairs={{0,8},{8,0},{16,24},{24,16},{32,40},{40,32},{48,56},{56,48},{64,72... | collective-permute-start | bytes 393224 | tf_op jit(solution)/shard_map/ppermute | solution.py:25
  269.8 8.4 %copy-start.4 = (bf16[256,256]{0,1:T(8,128)(2,1)}, bf16[256,256]{0,1:T(8,128)(2,1)S(1)}, u32[]{:S(2)}) copy-start(bf16[256,256]{0,1:T(8,128)(2,1)S(1)} %collective-permute-done.2) | copy-start | bytes 393220
  269.9 8.4 %collective-permute-start.3 = (bf16[256,256]{0,1:T(8,128)(2,1)S(1)}, bf16[256,256]{0,1:T(8,128)(2,1)S(1)}, u32[]{:S(2)}, u32[]{:S(2)}) collective-permute-start(bf16[256,256]{0,1:T(8,128)(2,1)S(1)} %get-tuple-element.44), channel_id=1, source_target_pairs={{0,16},{8,24},{16,0},{24,8},{32,48},{40,56},{48,32},{56,40},{64,80... | collective-permute-start | bytes 393224 | tf_op jit(solution)/shard_map/ppermute | solution.py:25
  278.3 0.6 copy-start.7
  278.9 7.0 %collective-permute-start.4 = (bf16[256,256]{0,1:T(8,128)(2,1)S(1)}, bf16[256,256]{0,1:T(8,128)(2,1)}, u32[]{:S(2)}, u32[]{:S(2)}) collective-permute-start(bf16[256,256]{0,1:T(8,128)(2,1)S(1)} %get-tuple-element.39), channel_id=1, source_target_pairs={{0,32},{8,40},{16,48},{24,56},{32,0},{40,8},{48,16},{56,24},{64,96... | collective-permute-start | bytes 393224 | tf_op jit(solution)/shard_map/ppermute | solution.py:25
  287.0 0.7 copy-start.3
  292.7 1.0 copy-start.2
  293.7 139.7 %copy-start.6 = (pred[256,256]{1,0:T(8,128)(4,1)S(1)}, pred[256,256]{1,0:T(8,128)(4,1)}, u32[]{:S(2)}) copy-start(pred[256,256]{1,0:T(8,128)(4,1)} %iota_compare_fusion) | copy-start | bytes 196612
  385.5 51.0 %copy-start.14 = (s32[2]{0:T(128)S(1)}, s32[2]{0:T(128)}, u32[]{:S(2)}) copy-start(s32[2]{0:T(128)} %iota_multiply_fusion) | copy-start | bytes 28
  434.8 1.0 copy-start.1
  502.3 3.2 copy-start.8
Sparse Core Ops, SparseCore 0:
  229.4 31.3 all-gather.2
